TPU v7x, 256 devices: a whole 4x4x8 slice. The times are simulated.
256 devices in a mesh: width: 16 (over z, x_hi), chan: 16 (over y, x_lo, core).
Axes of the slice: x: 4 (x_hi: 2, x_lo: 2; x = x_hi * 2 + x_lo), y: 4, z: 8, core: 2. Of those that a mesh axis runs over, the one named last changes fastest.
Arguments:
- activations: bfloat16 [512, 2, 12288], P('chan', None, 'width'), may hold values from -6 to 6
- filters: bfloat16 [512, 3, 3, 512], P('chan'), may hold values from -0.125 to 0.125
- cotangent: bfloat16 [512, 2, 12288], P('chan', None, 'width'), may hold values from -6 to 6
Outputs:
- conv_output: bfloat16 [512, 2, 12288], P('chan', None, 'width')
- input_grad: bfloat16 [512, 2, 12288], P('chan', None, 'width')
- filter_grad: float32 [512, 3, 3, 512], P('chan')
All inputs are finite; a program needn't handle non-finite values.
Results may differ from a plain program's by a relative error of at most 0.001.
Values may be sent and summed in bfloat16 or wider, within the bound.
A program may use at most 128 MiB of HBM per device.

v0:
```python
import math
import jax
import jax.numpy as jnp
from jax import lax
from jax.sharding import PartitionSpec as P


def padded_2(shard, sides, width):
    for axis, dim in sides:
        devices, length = (lax.axis_size(axis), shard.shape[dim])
        up = [(i, (i + 1) % devices) for i in range(devices - 1)]
        down = [(j, i) for i, j in up]
        last = lax.slice_in_dim(shard, length - width, length, axis=dim)
        leading = lax.slice_in_dim(shard, 0, width, axis=dim)
        before = lax.ppermute(last, axis, up)
        after = lax.ppermute(leading, axis, down)
        shard = jnp.concatenate([before, shard, after], axis=dim)
    return shard


def pad_rows(field):
    return jnp.pad(field, ((0, 0), (1, 1), (0, 0)))


def stack_taps(padded, rows, cols, flipped):
    pieces = []
    for tap_row in range(3):
        for tap_col in range(3):
            first_row = 2 - tap_row if flipped else tap_row
            first_col = 2 - tap_col if flipped else tap_col
            pieces.append(
                padded[:, first_row : first_row + rows, first_col : first_col + cols].reshape(
                    padded.shape[0], rows * cols
                )
            )
    return jnp.concatenate(pieces, 0)


def tap_major(block):
    number_in = block.shape[0]
    number_out = block.shape[3]
    return jnp.transpose(block, (1, 2, 0, 3)).reshape(9 * number_in, number_out)


def body(activations, filters, cotangent):
    cin_dev, rows, cols = activations.shape
    cout_dev = cotangent.shape[0]
    edged = padded_2(activations, (("width", 2),), 1)
    source_stack = stack_taps(pad_rows(edged), rows, cols, False)
    block = tap_major(filters)
    summed = lax.dot_general(
        block, source_stack, (((0,), (0,)), ((), ())), preferred_element_type=jnp.float32
    )
    forward = lax.psum_scatter(
        summed.reshape(cout_dev * lax.axis_size("chan"), rows, cols),
        "chan",
        scatter_dimension=0,
        tiled=True,
    )
    conv_output = forward.astype(jnp.bfloat16)
    grad_edged = padded_2(cotangent, (("width", 2),), 1)
    shards = lax.all_gather(grad_edged, "chan", axis=0, tiled=True)
    number_rows = shards.shape[0]
    block = filters.reshape(cin_dev, 9 * number_rows)
    grad_stack = stack_taps(pad_rows(shards), rows, cols, True)
    input_sum = jnp.dot(block, grad_stack, preferred_element_type=jnp.float32)
    interior = shards[:, :, 1:-1].reshape(number_rows, rows * cols)
    tap_grads = lax.dot_general(
        source_stack, interior, (((1,), (1,)), ((), ())), preferred_element_type=jnp.float32
    )
    tap_grads = jnp.transpose(tap_grads.reshape(3, 3, cin_dev, number_rows), (2, 0, 1, 3))
    filter_sum = tap_grads
    input_sum, filter_sum = (input_sum, filter_sum)
    filter_total = lax.psum(filter_sum, "width")
    factor = 1.0 / math.sqrt(rows * cols * lax.axis_size("width"))
    input_grad = input_sum.reshape(cin_dev, rows, cols).astype(jnp.bfloat16)
    return (conv_output, input_grad, filter_total * factor)


def solution(mesh):
    in_specs = (P("chan", None, "width"), P("chan", None, None, None), P("chan", None, "width"))
    out_specs = (P("chan", None, "width"), P("chan", None, "width"), P("chan", None, None, None))
    return jax.shard_map(body, mesh=mesh, in_specs=in_specs, out_specs=out_specs, check_vma=False)
```

profile of v0, /device:TPU:8, one launch (start us, length us, event | category | flops | bytes accessed | tf_op | source)
XLA Modules:
  0.0 344.5 jit_solution(17910656039230067917)
XLA Ops:
  7.2 0.9 fusion.8
  8.1 4.9 %collective-permute-start.2 = (bf16[32,2,1]{2,1,0:T(2,128)(2,1)S(1)}, bf16[32,2,1]{2,1,0:T(2,128)(2,1)S(1)}, u32[]{:S(2)}, u32[]{:S(2)}) collective-permute-start(bf16[32,2,1]{2,1,0:T(2,128)(2,1)S(1)} %get-tuple-element.18), channel_id=1, source_target_pairs={{0,16},{16,32},{32,48},{48,64},{64,80},{80,96},{96,112},{112,128},... | collective-permute-start | bytes 392 | tf_op jit(solution)/shard_map/ppermute | solution.py:15
  13.0 1.3 collective-permute-start.3
  14.3 0.8 fusion.9
  15.2 6.1 %collective-permute-start = (bf16[32,2,1]{2,1,0:T(2,128)(2,1)S(1)}, bf16[32,2,1]{2,1,0:T(2,128)(2,1)S(1)}, u32[]{:S(2)}, u32[]{:S(2)}) collective-permute-start(bf16[32,2,1]{2,1,0:T(2,128)(2,1)S(1)} %get-tuple-element.22), channel_id=1, source_target_pairs={{0,16},{16,32},{32,48},{48,64},{64,80},{80,96},{96,112},{112,128},... | collective-permute-start | bytes 392 | tf_op jit(solution)/shard_map/ppermute | solution.py:15
  21.2 1.3 collective-permute-start.1
  22.5 1.2 copy.10
  23.8 0.4 reshape.94
  24.2 0.6 dynamic-slice
  25.5 0.9 pad_maximum_fusion
  26.4 1.9 collective-permute-done.1
  28.4 0.4 select_maximum_fusion
  28.7 0.6 fusion.7
  30.4 1.0 fusion.10
  31.4 3.5 %copy.9 = f32[512,2,768]{2,1,0:T(2,128)} copy(f32[512,2,768]{0,2,1:T(8,128)S(1)} %bitcast.58) | data formatting | bytes 6291456 | tf_op jit(solution)/shard_map/reshape | solution.py:55
  34.9 80.9 %all-reduce.7 = bf16[512,2,768]{2,1,0:T(2,128)(2,1)S(1)} all-reduce(f32[512,2,768]{2,1,0:T(2,128)} %copy.9), channel_id=2, replica_groups=mesh['width'=16,'chan'=16] {'chan'}, use_global_device_ids=true, to_apply=%region_0.1.clone | all-reduce | flops 786432 | bytes 4718592
  115.8 0.7 dynamic-slice_convert_fusion
  116.5 33.4 %pad_slice_fusion = (bf16[512,2,768]{2,1,0:T(2,128)(2,1)}, bf16[512,2,768]{2,1,0:T(2,128)(2,1)S(1)}, bf16[512,2,768]{2,1,0:T(2,128)(2,1)S(1)}, bf16[512,2,768]{2...) fusion(bf16[512,2,770]{2,1,0:T(2,128)(2,1)} %all-gather.2.clone, ...), kind=kLoop, calls=%fused_computation | loop fusion | bytes 20709376 | tf_op jit(solution)/shard_map/slice | solution.py:32
  150.2 1.3 constant_dynamic-update-slice_fusion.17
  151.4 1.4 copy.22
  152.9 1.4 copy.23
  154.3 1.4 copy.24
  155.7 1.9 reshape.95
  157.6 1.4 copy.25
  159.0 0.5 copy-done.7
  159.5 1.4 copy.26
  160.9 0.5 copy-done.6
  161.4 1.4 copy.27
  163.1 1.1 copy-done.5
  164.5 0.9 copy-done.9
  165.4 0.5 copy-done.10
  165.9 1.5 fusion.3
  167.4 2.8 constant_dynamic-update-slice_fusion.16
  170.2 1.3 constant_dynamic-update-slice_fusion.15
  171.4 0.7 copy-done.2
  172.2 1.3 constant_dynamic-update-slice_fusion.14
  173.4 0.7 copy-done.3
  174.1 1.2 constant_dynamic-update-slice_fusion.13
  175.4 0.7 copy-done.1
  176.1 1.3 constant_dynamic-update-slice_fusion.12
  177.4 0.6 copy-done
  178.1 1.2 constant_dynamic-update-slice_fusion.11
  179.3 1.3 constant_dynamic-update-slice_fusion.10
  180.6 1.3 constant_dynamic-update-slice_fusion.9
  181.9 7.5 %fusion = bf16[32,1536]{1,0:T(8,128)(2,1)S(1)} fusion(bf16[32,4608]{1,0:T(8,128)(2,1)S(1)} %reshape.94, bf16[4608,1536]{1,0:T(8,128)(2,1)} %constant_dynamic-update-slice_fusion.9), kind=kOutput, calls=%fused_computation.7 | convolution fusion | flops 453033984 | bytes 14548992 | tf_op jit(solution)/shard_map/dot_general | solution.py:66
  189.4 0.7 convert_element_type.19
  190.1 145.6 %all-reduce.6.cloned.1.call-done = f32[32,3,3,512]{3,0,2,1:T(8,128)} async-done(((f32[32,3,3,512]{3,0,2,1:T(8,128)}), f32[32,3,3,512]{3,0,2,1:T(8,128)}) %all-reduce.6.cloned.1.call-update) | async-done | bytes 589840 | tf_op jit(solution)/shard_map/psum | solution.py:74
  335.7 1.9 broadcast_multiply_fusion
  (51 shorter events, 1.8 us)
Async XLA Ops:
  7.2 17.0 %copy-start.14 = (u32[256]{0:T(256)S(1)}, u32[256]{0:T(256)}, u32[]{:S(2)}) copy-start(u32[256]{0:T(256)} %constant.11) | copy-start | bytes 3076
  7.2 18.3 %copy-start.13 = (bf16[32,2,768]{2,1,0:T(2,128)(2,1)S(1)}, bf16[32,2,768]{2,1,0:T(2,128)(2,1)}, u32[]{:S(2)}) copy-start(bf16[32,2,768]{2,1,0:T(2,128)(2,1)} %param.5) | copy-start | bytes 294916
  7.2 17.0 %copy-start.12 = (bf16[32,2,768]{2,1,0:T(2,128)(2,1)S(1)}, bf16[32,2,768]{2,1,0:T(2,128)(2,1)}, u32[]{:S(2)}) copy-start(bf16[32,2,768]{2,1,0:T(2,128)(2,1)} %param.3) | copy-start | bytes 294916
  7.2 109.3 %all-gather.2.cloned.1.call-start = ((), (), s32[]{:S(2)}) async-start(), calls=%async_computation | async-start | bytes 1949696 | tf_op jit(solution)/shard_map/all_gather | solution.py:62
  8.1 17.3 %collective-permute-start.2 = (bf16[32,2,1]{2,1,0:T(2,128)(2,1)S(1)}, bf16[32,2,1]{2,1,0:T(2,128)(2,1)S(1)}, u32[]{:S(2)}, u32[]{:S(2)}) collective-permute-start(bf16[32,2,1]{2,1,0:T(2,128)(2,1)S(1)} %get-tuple-element.18), channel_id=1, source_target_pairs={{0,16},{16,32},{32,48},{48,64},{64,80},{80,96},{96,112},{112,128},... | collective-permute-start | bytes 392 | tf_op jit(solution)/shard_map/ppermute | solution.py:15
  13.0 12.4 %collective-permute-start.3 = (bf16[32,2,1]{2,1,0:T(2,128)(2,1)S(1)}, bf16[32,2,1]{2,1,0:T(2,128)(2,1)S(1)}, u32[]{:S(2)}, u32[]{:S(2)}) collective-permute-start(bf16[32,2,1]{2,1,0:T(2,128)(2,1)S(1)} %get-tuple-element.19), channel_id=1, source_target_pairs={{16,0},{32,16},{48,32},{64,48},{80,64},{96,80},{112,96},{128,112},... | collective-permute-start | bytes 392 | tf_op jit(solution)/shard_map/ppermute | solution.py:16
  15.2 11.3 %collective-permute-start = (bf16[32,2,1]{2,1,0:T(2,128)(2,1)S(1)}, bf16[32,2,1]{2,1,0:T(2,128)(2,1)S(1)}, u32[]{:S(2)}, u32[]{:S(2)}) collective-permute-start(bf16[32,2,1]{2,1,0:T(2,128)(2,1)S(1)} %get-tuple-element.22), channel_id=1, source_target_pairs={{0,16},{16,32},{32,48},{48,64},{64,80},{80,96},{96,112},{112,128},... | collective-permute-start | bytes 392 | tf_op jit(solution)/shard_map/ppermute | solution.py:15
  21.2 7.1 %collective-permute-start.1 = (bf16[32,2,1]{2,1,0:T(2,128)(2,1)S(1)}, bf16[32,2,1]{2,1,0:T(2,128)(2,1)S(1)}, u32[]{:S(2)}, u32[]{:S(2)}) collective-permute-start(bf16[32,2,1]{2,1,0:T(2,128)(2,1)S(1)} %get-tuple-element.23), channel_id=1, source_target_pairs={{16,0},{32,16},{48,32},{64,48},{80,64},{96,80},{112,96},{128,112},... | collective-permute-start | bytes 392 | tf_op jit(solution)/shard_map/ppermute | solution.py:16
  26.4 309.3 %all-reduce.6.cloned.1.call-start = ((), (), s32[]{:S(2)}) async-start(), calls=%async_computation.1 | async-start | bytes 1179648 | tf_op jit(solution)/shard_map/psum | solution.py:74
  29.4 1.0 copy-start.11
  30.0 1.4 copy-start.8
  157.6 1.9 copy-start.7
  159.5 1.9 copy-start.6
  162.8 1.4 copy-start.5
  164.2 1.2 copy-start.9
  164.2 1.7 copy-start.10
  167.4 2.8 copy-start.4
  170.2 2.0 copy-start.2
  172.1 2.0 copy-start.3
  174.1 2.0 copy-start.1
  176.1 2.0 copy-start
Sparse Core Ops, SparseCore 0:
  26.5 44.9 all-gather.1
  167.5 168.1 all-reduce.5
where the time goes:
time: 345 us; the launch traced here: 344 us
  waiting for transfers between devices  148 us (43%)
  blocking collectives  80.9 us (23%)
  local copies, waits for them, and re-layouts  73.8 us (21%)
  between operations  15.1 us (4%)
  starting transfers between devices  13.6 us (4%)
  matrix products  9.99 us (3%)
  other arithmetic  3.53 us (1%)
    psum x1, waiting for transfers between devices, body(): filter_total = lax.psum(filter_sum, 'width')  146 us
    unnamed x1, blocking collectives  80.9 us
    slice x2, local copies, waits for them, and re-layouts, stack_taps(): padded[:, first_row:first_row + rows, first_col:first_col + cols]  34 us
    unnamed x66, local copies, waits for them, and re-layouts  29.6 us
    ppermute x2, starting transfers between devices, padded_2(): before = lax.ppermute(last, axis, up)  11 us
    dot_general x1, matrix products, body(): input_sum = jnp.dot(block, grad_stack, preferred_element_type=jnp.float32)  7.52 us
  transfers between devices with their start and end apart: 6, of which 2 were waited for; matrix products, arithmetic and copies ran while one was open for 9% of the time, Pallas kernels for 0%

commit v1 on v0

--- a/solution.py
+++ b/solution.py
@@ -71,7 +71,7 @@
     tap_grads = jnp.transpose(tap_grads.reshape(3, 3, cin_dev, number_rows), (2, 0, 1, 3))
     filter_sum = tap_grads
     input_sum, filter_sum = (input_sum, filter_sum)
-    filter_total = lax.psum(filter_sum, "width")
+    filter_total = lax.all_gather(filter_sum, "width").sum(axis=0)
     factor = 1.0 / math.sqrt(rows * cols * lax.axis_size("width"))
     input_grad = input_sum.reshape(cin_dev, rows, cols).astype(jnp.bfloat16)
     return (conv_output, input_grad, filter_total * factor)

time: 345 us -> 292 us (0.85); the launches traced: 344 us -> 287 us
  waiting for transfers between devices: 148 us -> 87.3 us
  blocking collectives: 80.9 us -> 102 us
  local copies, waits for them, and re-layouts: 73.8 us -> 53.1 us
  other arithmetic: 3.53 us -> 9.12 us
    psum x1 -> x0, waiting for transfers between devices: 146 us -> none  [body(): filter_total = lax.psum(filter_sum, 'width')]
    all_gather x0 -> x1, waiting for transfers between devices: none -> 52.8 us  [body(): filter_total = lax.all_gather(filter_sum, 'width').sum(axis=0)]
    all_gather x1, waiting for transfers between devices: 0.01 us -> 23.8 us  [body(): shards = lax.all_gather(grad_edged, 'chan', axis=0, tiled=True)]
    unnamed x1, blocking collectives: 80.9 us -> 102 us
    unnamed x66 -> x64, local copies, waits for them, and re-layouts: 29.6 us -> 10.1 us
    ppermute x2, waiting for transfers between devices: 1.92 us -> 10.6 us  [padded_2(): after = lax.ppermute(leading, axis, down)]
    dot_general x1, matrix products: 7.52 us -> 2.5 us  [body(): input_sum = jnp.dot(block, grad_stack, preferred_element_type=jnp.float32)]
    reduce_sum x0 -> x1, other arithmetic: none -> 4.84 us  [body(): filter_total = lax.all_gather(filter_sum, 'width').sum(axis=0)]
  transfers between devices with their start and end apart: 6 -> 6, of which waited for: 2 -> 5; matrix products, arithmetic and copies ran while one was open for 9% -> 6% of each run, Pallas kernels for 0% -> 0%
where the time goes in v1:
time: 292 us; the launch traced here: 287 us
  blocking collectives  102 us (35%)
  waiting for transfers between devices  87.3 us (30%)
  local copies, waits for them, and re-layouts  53.1 us (18%)
  between operations  15.2 us (5%)
  starting transfers between devices  12.3 us (4%)
  other arithmetic  9.12 us (3%)
  matrix products  7.66 us (3%)
    unnamed x1, blocking collectives  102 us
    all_gather x1, waiting for transfers between devices, body(): filter_total = lax.all_gather(filter_sum, 'width').sum(axis=0)  52.8 us
    slice x2, local copies, waits for them, and re-layouts, stack_taps(): padded[:, first_row:first_row + rows, first_col:first_col + cols]  33.9 us
    all_gather x1, waiting for transfers between devices, body(): shards = lax.all_gather(grad_edged, 'chan', axis=0, tiled=True)  23.8 us
    ppermute x2, waiting for transfers between devices, padded_2(): after = lax.ppermute(leading, axis, down)  10.6 us
    unnamed x64, local copies, waits for them, and re-layouts  10.1 us
    ppermute x2, starting transfers between devices, padded_2(): before = lax.ppermute(last, axis, up)  9.6 us
  transfers between devices with their start and end apart: 6, of which 5 were waited for; matrix products, arithmetic and copies ran while one was open for 6% of the time, Pallas kernels for 0%

profile of v1, /device:TPU:8, one launch (start us, length us, event | category | flops | bytes accessed | tf_op | source)
XLA Modules:
  0.0 287.1 jit_solution(6758565142396160245)
XLA Ops:
  7.2 0.8 fusion.8
  8.1 4.9 %collective-permute-start.2 = (bf16[32,2,1]{2,1,0:T(2,128)(2,1)S(1)}, bf16[32,2,1]{2,1,0:T(2,128)(2,1)S(1)}, u32[]{:S(2)}, u32[]{:S(2)}) collective-permute-start(bf16[32,2,1]{2,1,0:T(2,128)(2,1)S(1)} %get-tuple-element.18), channel_id=1, source_target_pairs={{0,16},{16,32},{32,48},{48,64},{64,80},{80,96},{96,112},{112,128},... | collective-permute-start | bytes 392 | tf_op jit(solution)/shard_map/ppermute | solution.py:15
  13.0 1.3 collective-permute-start.3
  14.3 0.1 collective-permute-done.2
  14.4 5.7 %collective-permute-done.3 = bf16[32,2,1]{2,1,0:T(2,128)(2,1)S(1)} collective-permute-done((bf16[32,2,1]{2,1,0:T(2,128)(2,1)S(1)}, bf16[32,2,1]{2,1,0:T(2,128)(2,1)S(1)}, u32[]{:S(2)}, u32[]{:S(2)}) %collective-permute-start.3) | collective-permute-done | bytes 160 | tf_op jit(solution)/shard_map/ppermute | solution.py:16
  20.1 1.8 pad_maximum_fusion
  22.0 0.8 fusion.9
  22.8 4.7 %collective-permute-start = (bf16[32,2,1]{2,1,0:T(2,128)(2,1)S(1)}, bf16[32,2,1]{2,1,0:T(2,128)(2,1)S(1)}, u32[]{:S(2)}, u32[]{:S(2)}) collective-permute-start(bf16[32,2,1]{2,1,0:T(2,128)(2,1)S(1)} %get-tuple-element.22), channel_id=1, source_target_pairs={{0,16},{16,32},{32,48},{48,64},{64,80},{80,96},{96,112},{112,128},... | collective-permute-start | bytes 392 | tf_op jit(solution)/shard_map/ppermute | solution.py:15
  27.5 1.3 collective-permute-start.1
  28.8 0.9 copy.16
  29.7 4.9 %collective-permute-done.1 = bf16[32,2,1]{2,1,0:T(2,128)(2,1)S(1)} collective-permute-done((bf16[32,2,1]{2,1,0:T(2,128)(2,1)S(1)}, bf16[32,2,1]{2,1,0:T(2,128)(2,1)S(1)}, u32[]{:S(2)}, u32[]{:S(2)}) %collective-permute-start.1) | collective-permute-done | bytes 160 | tf_op jit(solution)/shard_map/ppermute | solution.py:16
  34.6 1.3 select_maximum_fusion
  35.9 0.6 fusion.7
  36.6 0.3 pad_maximum_fusion.1
  37.2 23.8 %all-gather.4.cloned.1.call-done = bf16[512,2,770]{2,1,0:T(2,128)(2,1)} async-done(((bf16[32,2,770]{2,1,0:T(2,128)(2,1)}), bf16[512,2,770]{2,1,0:T(2,128)(2,1)}) %all-gather.4.cloned.1.call-update) | async-done | bytes 1576976 | tf_op jit(solution)/shard_map/all_gather | solution.py:62
  60.9 33.3 %pad_slice_fusion = (bf16[512,2,768]{2,1,0:T(2,128)(2,1)}, bf16[512,2,768]{2,1,0:T(2,128)(2,1)}, bf16[512,2,768]{2,1,0:T(2,128)(2,1)}, bf16[512,2,768]{2,1,0:T(2...) fusion(bf16[512,2,770]{2,1,0:T(2,128)(2,1)} %all-gather.4.clone, ...), kind=kLoop, calls=%fused_computation | loop fusion | bytes 20709376 | tf_op jit(solution)/shard_map/slice | solution.py:32
  94.3 2.0 reshape.96
  96.2 2.9 %fusion.3 = f32[32,3,3,512]{3,0,2,1:T(8,128)} fusion(bf16[3,3,32,1536]{3,2,1,0:T(8,128)(2,1)S(1)} %bitcast.79, bf16[512,1536,1,1]{1,0,2,3:T(8,128)(2,1)} %reshape.96), kind=kOutput, calls=%fused_computation.10 | convolution fusion | flops 452984832 | bytes 3047424 | tf_op jit(solution)/shard_map/dot_general | solution.py:68
  99.2 0.3 copy.10
  99.5 0.4 reshape.94
  99.9 0.6 dynamic-slice
  101.1 2.2 fusion.10
  103.4 3.6 %copy.9 = f32[512,2,768]{2,1,0:T(2,128)} copy(f32[512,2,768]{0,2,1:T(8,128)S(1)} %bitcast.59) | data formatting | bytes 6291456 | tf_op jit(solution)/shard_map/reshape | solution.py:55
  107.0 102.5 %all-reduce.4 = bf16[512,2,768]{2,1,0:T(2,128)(2,1)S(1)} all-reduce(f32[512,2,768]{2,1,0:T(2,128)} %copy.9), channel_id=3, replica_groups=mesh['width'=16,'chan'=16] {'chan'}, use_global_device_ids=true, to_apply=%region_0.1.clone | all-reduce | flops 786432 | bytes 4718592
  209.5 0.7 dynamic-slice_convert_fusion
  210.2 0.3 copy.21
  210.4 0.4 copy-done.8
  210.9 0.3 copy.22
  211.2 0.8 copy-done.7
  212.0 0.3 copy.23
  212.2 0.5 copy-done.6
  212.7 0.3 copy.24
  212.9 0.8 copy-done.1
  213.7 0.3 copy.25
  214.0 0.5 copy-done.5
  214.5 0.3 copy.26
  214.8 0.8 copy-done.4
  215.5 0.3 copy.27
  215.8 0.5 copy-done.3
  216.3 0.3 copy.28
  216.5 0.8 copy-done.2
  217.3 0.3 copy.29
  217.7 0.1 constant_dynamic-update-slice_fusion.16
  218.6 2.5 fusion
  221.1 0.7 convert_element_type.19
  221.8 52.8 %all-gather.6.cloned.1.call-done = f32[512,3,3,512]{3,0,2,1:T(8,128)} async-done(((f32[32,3,3,512]{3,0,2,1:T(8,128)}), f32[512,3,3,512]{3,0,2,1:T(8,128)}) %all-gather.6.cloned.1.call-update) | async-done | bytes 9437200 | tf_op jit(solution)/shard_map/all_gather | solution.py:74
  274.5 4.8 %reduce_sum.9 = f32[32,3,3,512]{3,0,2,1:T(8,128)S(1)} reduce(f32[16,32,3,3,512]{4,1,0,3,2:T(8,128)} %bitcast.61, f32[]{:T(128)} %constant.2.clone.1), dimensions={0}, to_apply=%region_1.2 | reduce | flops 2211840 | bytes 10027012 | tf_op jit(solution)/shard_map/reduce_sum | solution.py:74
  279.4 0.9 broadcast_multiply_fusion
  (50 shorter events, 1.2 us)
Async XLA Ops:
  7.2 29.4 %copy-start.12 = (bf16[32,2,768]{2,1,0:T(2,128)(2,1)S(1)}, bf16[32,2,768]{2,1,0:T(2,128)(2,1)}, u32[]{:S(2)}) copy-start(bf16[32,2,768]{2,1,0:T(2,128)(2,1)} %param.3) | copy-start | bytes 294916
  7.2 53.8 %all-gather.4.cloned.1.call-start = ((), (), s32[]{:S(2)}) async-start(), calls=%async_computation | async-start | bytes 1949696 | tf_op jit(solution)/shard_map/all_gather | solution.py:62
  8.1 6.4 %collective-permute-start.2 = (bf16[32,2,1]{2,1,0:T(2,128)(2,1)S(1)}, bf16[32,2,1]{2,1,0:T(2,128)(2,1)S(1)}, u32[]{:S(2)}, u32[]{:S(2)}) collective-permute-start(bf16[32,2,1]{2,1,0:T(2,128)(2,1)S(1)} %get-tuple-element.18), channel_id=1, source_target_pairs={{0,16},{16,32},{32,48},{48,64},{64,80},{80,96},{96,112},{112,128},... | collective-permute-start | bytes 392 | tf_op jit(solution)/shard_map/ppermute | solution.py:15
  13.0 7.1 %collective-permute-start.3 = (bf16[32,2,1]{2,1,0:T(2,128)(2,1)S(1)}, bf16[32,2,1]{2,1,0:T(2,128)(2,1)S(1)}, u32[]{:S(2)}, u32[]{:S(2)}) collective-permute-start(bf16[32,2,1]{2,1,0:T(2,128)(2,1)S(1)} %get-tuple-element.19), channel_id=1, source_target_pairs={{16,0},{32,16},{48,32},{64,48},{80,64},{96,80},{112,96},{128,112},... | collective-permute-start | bytes 392 | tf_op jit(solution)/shard_map/ppermute | solution.py:16
  21.9 252.6 %all-gather.6.cloned.1.call-start = ((), (), s32[]{:S(2)}) async-start(), calls=%async_computation.1 | async-start | bytes 10027008 | tf_op jit(solution)/shard_map/all_gather | solution.py:74
  22.8 6.9 %collective-permute-start = (bf16[32,2,1]{2,1,0:T(2,128)(2,1)S(1)}, bf16[32,2,1]{2,1,0:T(2,128)(2,1)S(1)}, u32[]{:S(2)}, u32[]{:S(2)}) collective-permute-start(bf16[32,2,1]{2,1,0:T(2,128)(2,1)S(1)} %get-tuple-element.22), channel_id=1, source_target_pairs={{0,16},{16,32},{32,48},{48,64},{64,80},{80,96},{96,112},{112,128},... | collective-permute-start | bytes 392 | tf_op jit(solution)/shard_map/ppermute | solution.py:15
  27.5 7.1 %collective-permute-start.1 = (bf16[32,2,1]{2,1,0:T(2,128)(2,1)S(1)}, bf16[32,2,1]{2,1,0:T(2,128)(2,1)S(1)}, u32[]{:S(2)}, u32[]{:S(2)}) collective-permute-start(bf16[32,2,1]{2,1,0:T(2,128)(2,1)S(1)} %get-tuple-element.23), channel_id=1, source_target_pairs={{16,0},{32,16},{48,32},{64,48},{80,64},{96,80},{112,96},{128,112},... | collective-permute-start | bytes 392 | tf_op jit(solution)/shard_map/ppermute | solution.py:16
  37.2 59.1 %copy-start.10 = (bf16[288,1536]{1,0:T(8,128)(2,1)}, bf16[288,1536]{1,0:T(8,128)(2,1)S(1)}, u32[]{:S(2)}) copy-start(bf16[288,1536]{1,0:T(8,128)(2,1)S(1)} %constant_dynamic-update-slice_fusion) | copy-start | bytes 2654212
  94.3 4.9 %copy-start = (bf16[512,2,768]{2,1,0:T(2,128)(2,1)}, bf16[512,2,768]{2,1,0:T(2,128)(2,1)S(1)}, u32[]{:S(2)}) copy-start(bf16[512,2,768]{2,1,0:T(2,128)(2,1)S(1)} %get-tuple-element.9) | copy-start | bytes 4718596
  96.2 3.0 %copy-start.11 = (bf16[32,3,3,512]{3,0,2,1:T(8,128)(2,1)S(1)}, bf16[32,3,3,512]{3,0,2,1:T(8,128)(2,1)}, u32[]{:S(2)}) copy-start(bf16[32,3,3,512]{3,0,2,1:T(8,128)(2,1)} %param.4) | copy-start | bytes 884740
  96.2 3.6 %copy-start.13 = (u32[256]{0:T(256)S(1)}, u32[256]{0:T(256)}, u32[]{:S(2)}) copy-start(u32[256]{0:T(256)} %constant.13) | copy-start | bytes 3076
  107.0 103.2 %copy-start.9 = (bf16[512,2,768]{2,1,0:T(2,128)(2,1)S(1)}, bf16[512,2,768]{2,1,0:T(2,128)(2,1)}, u32[]{:S(2)}) copy-start(bf16[512,2,768]{2,1,0:T(2,128)(2,1)} %get-tuple-element.11) | copy-start | bytes 4718596
  209.4 1.4 copy-start.8
  210.4 1.5 copy-start.7
  211.1 1.5 copy-start.6
  212.2 1.5 copy-start.1
  212.9 1.6 copy-start.5
  214.0 1.5 copy-start.4
  214.8 1.5 copy-start.3
  215.8 1.5 copy-start.2
Sparse Core Ops, SparseCore 0:
  22.0 38.8 all-gather.3
  99.3 175.1 all-gather.5
